TPU v7x, 32 devices: a whole 2x2x4 slice. The times are simulated.
32 devices in a mesh: groups: 2 (over x), vel: 16 (over z, y, core).
Axes of the slice: x: 2, y: 2, z: 4, core: 2. Of those that a mesh axis runs over, the one named last changes fastest.
Arguments:
- epoch_maps: bfloat16 [128, 192, 512], P('vel', 'groups'), parts along dimension 1, may hold values from -6 to 6, as said below
- velocity: int32 [16, 2], P('vel'), may hold values from -16 to 16, as said below
- slot_epoch: int32 [64], replicated, may hold values from 0 to 63, each once
- epoch_time: int32 [64], replicated, may hold values from 0 to 127, as said below
Outputs:
- likelihood: float32 [16, 192, 512], P('vel', 'groups'), parts along dimension 1
- best_value: float32 [192, 512], P('groups'), parts along dimension 0
There are 2 independent parts, one for each index of `groups`. A program takes and returns all parts, laid end to end along the dimension named above; an argument that names none is the same for every part. Nothing has to cross between parts.
Inputs may be any that keep to these rules, and one draw needn't show every extreme that they name: `epoch_maps`: the first 64 images are likelihoods, the others weights of at least 0.25 and at most 4. `velocity`: all rows are distinct; rows (16, 16) and (-16, -16) both occur. `epoch_time`: strictly increasing, the first 0 and the last 127. `slot_epoch`: each epoch stands in exactly one slot.
All inputs are finite; a program needn't handle non-finite values.
Results may differ from a plain program's by a relative error of at most 0.0029.
Values may be sent and summed in bfloat16 or wider, within the bound.
A program may use at most 64 MiB of HBM per device.

v0:
```python
import math

import jax
import jax.numpy as jnp
import numpy as np
from jax import lax
from jax.sharding import PartitionSpec as P

SPLINE = np.array(
    [
        [64.0, 256.0, 64.0, 0.0],
        [27.0, 235.0, 121.0, 1.0],
        [8.0, 184.0, 184.0, 8.0],
        [1.0, 121.0, 235.0, 27.0],
    ],
    np.float32,
)
spline_norm = 147456.0
rate_divisor = 32


def spline_taps(offset):
    whole_shift = offset // 4
    fraction = offset - 4 * whole_shift
    weights = []
    for tap_number in range(4):
        tap_value = jnp.zeros(offset.shape, jnp.float32)
        for fraction_level in range(4):
            tap_value = tap_value + jnp.where(
                fraction == fraction_level, float(SPLINE[fraction_level, tap_number]), 0.0
            )
        weights.append(tap_value)
    return (whole_shift, weights)


def band_matrix(whole_shift, weights, length):
    outputs = lax.broadcasted_iota(jnp.int32, (length, length), 0)
    inputs = lax.broadcasted_iota(jnp.int32, (length, length), 1)
    distance = inputs[None, None] - outputs[None, None] - whole_shift[:, :, None, None] + 1
    matrix = jnp.zeros(distance.shape, jnp.float32)
    for tap_number in range(4):
        matrix = matrix + jnp.where(
            distance == tap_number, weights[tap_number][:, :, None, None], 0.0
        )
    return matrix.astype(jnp.bfloat16)


def lookup_times(slot_ids, slot_time):
    epochs = slot_time.shape[0]
    table = (
        slot_ids[:, None] == lax.broadcasted_iota(jnp.int32, (slot_ids.shape[0], epochs), 1)
    ).astype(jnp.int32)
    return jnp.sum(table * slot_time[None, :], axis=1)


def shift_bands(times, rate_rows, rows_length, columns_length):
    row_whole, row_weights = spline_taps(times[:, None] * rate_rows[None, :, 0] // rate_divisor)
    column_whole, column_weights = spline_taps(
        times[:, None] * rate_rows[None, :, 1] // rate_divisor
    )
    return (
        band_matrix(row_whole, row_weights, rows_length),
        band_matrix(column_whole, column_weights, columns_length),
    )


def local(epoch_maps, velocity, slot_epoch, epoch_time):
    epochs = slot_epoch.shape[0]
    slot_time = lookup_times(slot_epoch, epoch_time)
    rows_length = epoch_maps.shape[1]
    columns_length = epoch_maps.shape[2]
    local_velocities = velocity.shape[0]
    initial = jnp.zeros((local_velocities, 2, rows_length, columns_length), jnp.float32)
    gathered = lax.all_gather(epoch_maps, "vel", axis=0, tiled=True)
    paired = gathered.reshape(2, epochs, rows_length, columns_length)
    block_size = math.gcd(epochs, 8)

    def one_block(block_index, running):
        block_first = block_index * block_size
        images = lax.dynamic_slice_in_dim(paired, block_first, block_size, 1)
        block_times = lax.dynamic_slice_in_dim(slot_time, block_first, block_size, 0)
        row_band, column_band = shift_bands(block_times, velocity, rows_length, columns_length)
        rows_done = jnp.einsum(
            "pvoi,mpij->pvmoj", row_band, images, preferred_element_type=jnp.float32
        ).astype(jnp.bfloat16)
        return running + jnp.einsum(
            "pvmoj,pvcj->vmoc", rows_done, column_band, preferred_element_type=jnp.float32
        )

    totals = lax.fori_loop(0, epochs // block_size, one_block, initial)
    stack_sums = totals / spline_norm
    likelihood = stack_sums[:, 0] / jnp.sqrt(stack_sums[:, 1] + 1.0)
    best_value = lax.pmax(jnp.max(likelihood, axis=0), "vel")
    return (likelihood, best_value)


def solution(mesh):
    return jax.shard_map(
        local,
        mesh=mesh,
        in_specs=(P("vel", "groups", None), P("vel", None), P(), P()),
        out_specs=(P("vel", "groups", None), P("groups", None)),
        check_vma=False,
    )
```

profile of v0, /device:TPU:0, one launch (start us, length us, event | category | flops | bytes accessed | tf_op | source)
XLA Modules:
  0.0 283.9 jit_solution(15816745322282400095)
XLA Ops:
  8.8 104.6 %all-gather.2.cloned.1.call-done = bf16[128,96,512]{2,1,0:T(8,128)(2,1)} async-done(((bf16[8,96,512]{2,1,0:T(8,128)(2,1)}), bf16[128,96,512]{2,1,0:T(8,128)(2,1)}) %all-gather.2.cloned.1.call-update) | async-done | bytes 12582928 | tf_op jit(solution)/shard_map/all_gather | solution.py:74
  113.4 71.9 %while.17 = (s32[]{:T(128)}, f32[1,2,96,512]{3,2,1,0:T(8,128)S(1)}, bf16[2,64,96,512]{3,2,1,0:T(8,128)(2,1)}, s32[64]{0:T(128)S(1)}, s32[1,2]{1,0:T(1,128)}, /*index=5*/s32[]{:T(128)}, s32[]{:T(128)}, s32[]{:T(128)}, s32[]{:T(128)}) while((s32[]{:T(128)}, f32[1,2,96,512]{3,2,1,0:T(8,128)S(1)}, bf16[2,64,96,512]{3,2,1,0:T(8,128)(2,1)}, ...), condition=%wide.region_2.3_spmd.clone, body=%wide.region_1.2_spmd.clone.sunk | while | flops 987949120 | bytes 4531293 | solution.py:90
  114.8 1.4 and_select_fusion.7
  116.3 6.1 %fusion.86 = f32[1,2,96,512]{3,2,1,0:T(8,128)S(1)} fusion(f32[8]{0:T(128)S(1)} %get-tuple-element.275, f32[8]{0:T(128)S(1)} %get-tuple-element.276, f32[8]{0:T(128)S(1)} %get-tuple-element.277, f32[8]{0:T(128)S(1)} %get-tuple-element.278, s32[8]{0:T(128)S(1)} %get-tuple-element.279, s32[512,512]{1,0:T(8,128)S(1)} %iota_subtract_fusion.4, ...), kind=kOutput, calls=%fused_computation.12.clone.1 | convolution fusion | flops 987676672 | bytes 3445061 | tf_op jit(solution)/shard_map/while/body/eval_jaxpr/pvmoj,pvcj->vmoc/dot_general | solution.py:86
  122.4 1.3 fusion.85
  123.8 1.4 and_select_fusion.7
  125.3 6.1 %fusion.86 = f32[1,2,96,512]{3,2,1,0:T(8,128)S(1)} fusion(f32[8]{0:T(128)S(1)} %get-tuple-element.275, f32[8]{0:T(128)S(1)} %get-tuple-element.276, f32[8]{0:T(128)S(1)} %get-tuple-element.277, f32[8]{0:T(128)S(1)} %get-tuple-element.278, s32[8]{0:T(128)S(1)} %get-tuple-element.279, s32[512,512]{1,0:T(8,128)S(1)} %iota_subtract_fusion.4, ...), kind=kOutput, calls=%fused_computation.12.clone.1 | convolution fusion | flops 987676672 | bytes 3445061 | tf_op jit(solution)/shard_map/while/body/eval_jaxpr/pvmoj,pvcj->vmoc/dot_general | solution.py:86
  131.4 1.3 fusion.85
  132.8 1.4 and_select_fusion.7
  134.3 6.1 %fusion.86 = f32[1,2,96,512]{3,2,1,0:T(8,128)S(1)} fusion(f32[8]{0:T(128)S(1)} %get-tuple-element.275, f32[8]{0:T(128)S(1)} %get-tuple-element.276, f32[8]{0:T(128)S(1)} %get-tuple-element.277, f32[8]{0:T(128)S(1)} %get-tuple-element.278, s32[8]{0:T(128)S(1)} %get-tuple-element.279, s32[512,512]{1,0:T(8,128)S(1)} %iota_subtract_fusion.4, ...), kind=kOutput, calls=%fused_computation.12.clone.1 | convolution fusion | flops 987676672 | bytes 3445061 | tf_op jit(solution)/shard_map/while/body/eval_jaxpr/pvmoj,pvcj->vmoc/dot_general | solution.py:86
  140.4 1.3 fusion.85
  141.7 1.4 and_select_fusion.7
  143.3 6.1 %fusion.86 = f32[1,2,96,512]{3,2,1,0:T(8,128)S(1)} fusion(f32[8]{0:T(128)S(1)} %get-tuple-element.275, f32[8]{0:T(128)S(1)} %get-tuple-element.276, f32[8]{0:T(128)S(1)} %get-tuple-element.277, f32[8]{0:T(128)S(1)} %get-tuple-element.278, s32[8]{0:T(128)S(1)} %get-tuple-element.279, s32[512,512]{1,0:T(8,128)S(1)} %iota_subtract_fusion.4, ...), kind=kOutput, calls=%fused_computation.12.clone.1 | convolution fusion | flops 987676672 | bytes 3445061 | tf_op jit(solution)/shard_map/while/body/eval_jaxpr/pvmoj,pvcj->vmoc/dot_general | solution.py:86
  149.4 1.3 fusion.85
  150.7 1.4 and_select_fusion.7
  152.3 6.1 %fusion.86 = f32[1,2,96,512]{3,2,1,0:T(8,128)S(1)} fusion(f32[8]{0:T(128)S(1)} %get-tuple-element.275, f32[8]{0:T(128)S(1)} %get-tuple-element.276, f32[8]{0:T(128)S(1)} %get-tuple-element.277, f32[8]{0:T(128)S(1)} %get-tuple-element.278, s32[8]{0:T(128)S(1)} %get-tuple-element.279, s32[512,512]{1,0:T(8,128)S(1)} %iota_subtract_fusion.4, ...), kind=kOutput, calls=%fused_computation.12.clone.1 | convolution fusion | flops 987676672 | bytes 3445061 | tf_op jit(solution)/shard_map/while/body/eval_jaxpr/pvmoj,pvcj->vmoc/dot_general | solution.py:86
  159.7 1.4 and_select_fusion.7
  161.3 6.1 %fusion.86 = f32[1,2,96,512]{3,2,1,0:T(8,128)S(1)} fusion(f32[8]{0:T(128)S(1)} %get-tuple-element.275, f32[8]{0:T(128)S(1)} %get-tuple-element.276, f32[8]{0:T(128)S(1)} %get-tuple-element.277, f32[8]{0:T(128)S(1)} %get-tuple-element.278, s32[8]{0:T(128)S(1)} %get-tuple-element.279, s32[512,512]{1,0:T(8,128)S(1)} %iota_subtract_fusion.4, ...), kind=kOutput, calls=%fused_computation.12.clone.1 | convolution fusion | flops 987676672 | bytes 3445061 | tf_op jit(solution)/shard_map/while/body/eval_jaxpr/pvmoj,pvcj->vmoc/dot_general | solution.py:86
  168.7 1.4 and_select_fusion.7
  170.3 6.1 %fusion.86 = f32[1,2,96,512]{3,2,1,0:T(8,128)S(1)} fusion(f32[8]{0:T(128)S(1)} %get-tuple-element.275, f32[8]{0:T(128)S(1)} %get-tuple-element.276, f32[8]{0:T(128)S(1)} %get-tuple-element.277, f32[8]{0:T(128)S(1)} %get-tuple-element.278, s32[8]{0:T(128)S(1)} %get-tuple-element.279, s32[512,512]{1,0:T(8,128)S(1)} %iota_subtract_fusion.4, ...), kind=kOutput, calls=%fused_computation.12.clone.1 | convolution fusion | flops 987676672 | bytes 3445061 | tf_op jit(solution)/shard_map/while/body/eval_jaxpr/pvmoj,pvcj->vmoc/dot_general | solution.py:86
  177.7 1.4 and_select_fusion.7
  179.2 6.1 %fusion.86 = f32[1,2,96,512]{3,2,1,0:T(8,128)S(1)} fusion(f32[8]{0:T(128)S(1)} %get-tuple-element.275, f32[8]{0:T(128)S(1)} %get-tuple-element.276, f32[8]{0:T(128)S(1)} %get-tuple-element.277, f32[8]{0:T(128)S(1)} %get-tuple-element.278, s32[8]{0:T(128)S(1)} %get-tuple-element.279, s32[512,512]{1,0:T(8,128)S(1)} %iota_subtract_fusion.4, ...), kind=kOutput, calls=%fused_computation.12.clone.1 | convolution fusion | flops 987676672 | bytes 3445061 | tf_op jit(solution)/shard_map/while/body/eval_jaxpr/pvmoj,pvcj->vmoc/dot_general | solution.py:86
  186.2 89.3 %all-reduce.2.cloned.1.call-done = f32[96,512]{1,0:T(8,128)} async-done(((f32[96,512]{1,0:T(8,128)}), f32[96,512]{1,0:T(8,128)}) %all-reduce.2.cloned.1.call-update) | async-done | bytes 196624 | tf_op jit(solution)/shard_map/pmax | solution.py:93
  275.4 1.6 copy.33
  (52 shorter events, 9.1 us)
Async XLA Ops:
  7.2 106.3 %all-gather.2.cloned.1.call-start = ((), (), s32[]{:S(2)}) async-start(), calls=%async_computation | async-start | bytes 13369344 | tf_op jit(solution)/shard_map/all_gather | solution.py:74
  7.9 267.5 %all-reduce.2.cloned.1.call-start = ((), (), s32[]{:S(2)}) async-start(), calls=%async_computation.1 | async-start | bytes 393216 | tf_op jit(solution)/shard_map/pmax | solution.py:93
Sparse Core Ops, SparseCore 0:
  10.3 103.1 all-gather.1
  186.3 89.0 all-reduce.1
where the time goes:
time: 285 us; the launch traced here: 284 us
  waiting for transfers between devices  195 us (68%)
  matrix products  48.5 us (17%)
  between operations  14.1 us (5%)
  other arithmetic  13.9 us (5%)
  local copies, waits for them, and re-layouts  12.3 us (4%)
    all_gather x1, waiting for transfers between devices, local(): gathered = lax.all_gather(epoch_maps, 'vel', axis=0, tiled=True)  105 us
    pmax x1, waiting for transfers between devices, local(): best_value = lax.pmax(jnp.max(likelihood, axis=0), 'vel')  89.3 us
    dot_general x8, matrix products, one_block(): jnp.einsum('pvmoj,pvcj->vmoc', rows_done, column_band, preferred_element_...  48.5 us
    select_n x8, other arithmetic, shift_bands(): times[:, None] * rate_rows[None, :, 0] // rate_divisor  10.9 us
    slice x8, local copies, waits for them, and re-layouts, shift_bands(): rate_rows[None, :, 0]  10.7 us
  transfers between devices with their start and end apart: 2, of which 2 were waited for; matrix products, arithmetic and copies ran while one was open for 0% of the time, Pallas kernels for 0%

commit v1 on v0

v1 whole, which is shorter than its diff:
```python
import functools
import math

import jax
import jax.numpy as jnp
from jax import lax
from jax.experimental import pallas as pl
from jax.experimental.pallas import tpu as pltpu
from jax.sharding import PartitionSpec as P

SPLINE = (
    (64.0, 256.0, 64.0, 0.0),
    (27.0, 235.0, 121.0, 1.0),
    (8.0, 184.0, 184.0, 8.0),
    (1.0, 121.0, 235.0, 27.0),
)
spline_norm = 147456.0
rate_divisor = 32
HALO = 64
LANES = 128


def scalar_taps(offset):
    whole = offset >> 2
    fraction = offset & 3
    taps = []
    for tap in range(4):
        value = jnp.float32(SPLINE[3][tap])
        for level in range(3):
            value = jnp.where(fraction == level, jnp.float32(SPLINE[level][tap]), value)
        taps.append(value)
    return whole, taps


def band(distance, offset):
    whole, taps = scalar_taps(offset)
    relative = distance - whole
    out = jnp.where(relative == 3, taps[3], 0.0)
    for tap in (2, 1, 0):
        out = jnp.where(relative == tap, taps[tap], out)
    return out.astype(jnp.bfloat16)


def stack_one(rate_row, rate_col, times, padded, bands, rows_done, count, rows, cols):
    blocks = cols // LANES
    row_distance = (
        lax.broadcasted_iota(jnp.int32, (rows, rows), 1)
        - lax.broadcasted_iota(jnp.int32, (rows, rows), 0)
        + 1
    )
    col_distance = (
        lax.broadcasted_iota(jnp.int32, (2 * LANES, LANES), 0)
        - lax.broadcasted_iota(jnp.int32, (2 * LANES, LANES), 1)
        + (1 - HALO)
    )
    for s in range(count):
        row_band = band(row_distance, (rate_row * times(s)) >> 5)
        bands[pl.ds(s * 2 * LANES, 2 * LANES), :] = band(
            col_distance, (rate_col * times(s)) >> 5
        )
        rows_done[s] = jnp.dot(
            row_band, padded[s], preferred_element_type=jnp.float32
        ).astype(jnp.bfloat16)
    lhs = jnp.concatenate(
        [
            jnp.concatenate(
                [rows_done[s, :, b * LANES : (b + 2) * LANES] for s in range(count)], axis=1
            )
            for b in range(blocks)
        ],
        axis=0,
    )
    return jnp.dot(lhs, bands[...], preferred_element_type=jnp.float32)


def pad_images(images, padded, count, rows, cols):
    zeros = jnp.zeros((rows, HALO), jnp.bfloat16)
    for s in range(count):
        padded[s] = jnp.concatenate([zeros, images[s], zeros], axis=1)


def stack_kernel(count, rows, cols, vel_ref, time_ref, images, out, padded, bands, rows_done):
    pad_images(images, padded, count, rows, cols)
    hypotheses = out.shape[0]

    @pl.loop(0, hypotheses)
    def _(v):
        total = stack_one(
            vel_ref[v, 0],
            vel_ref[v, 1],
            lambda s: time_ref[s],
            padded,
            bands,
            rows_done,
            count,
            rows,
            cols,
        )
        for b in range(cols // LANES):
            out[v, :, b * LANES : (b + 1) * LANES] = total[b * rows : (b + 1) * rows].astype(
                out.dtype
            )


def local(n, epoch_maps, velocity, slot_epoch, epoch_time):
    count, rows, cols = epoch_maps.shape
    epochs = slot_epoch.shape[0]
    me = lax.axis_index("vel")
    vels = lax.all_gather(velocity, "vel", axis=0, tiled=True)
    first = lax.rem(me * count, epochs)
    slots = lax.dynamic_slice_in_dim(slot_epoch, first, count, 0)
    times = epoch_time[slots]
    partial = pl.pallas_call(
        functools.partial(stack_kernel, count, rows, cols),
        out_shape=jax.ShapeDtypeStruct((vels.shape[0], rows, cols), jnp.bfloat16),
        in_specs=[
            pl.BlockSpec(memory_space=pltpu.SMEM),
            pl.BlockSpec(memory_space=pltpu.SMEM),
            pl.BlockSpec(memory_space=pltpu.VMEM),
        ],
        out_specs=pl.BlockSpec(memory_space=pltpu.VMEM),
        scratch_shapes=[
            pltpu.VMEM((count, rows, cols + 2 * HALO), jnp.bfloat16),
            pltpu.VMEM((count * 2 * LANES, LANES), jnp.bfloat16),
            pltpu.VMEM((count, rows, cols + 2 * HALO), jnp.bfloat16),
        ],
    )(vels, times, epoch_maps)
    mine = velocity.shape[0]
    received = lax.all_to_all(partial, "vel", 0, 0, tiled=True)
    received = received.reshape(2, n // 2, mine, rows, cols)
    stack_sums = jnp.sum(received.astype(jnp.float32), axis=1) / spline_norm
    likelihood = stack_sums[0] / jnp.sqrt(stack_sums[1] + 1.0)
    best_value = lax.pmax(jnp.max(likelihood, axis=0), "vel")
    return (likelihood, best_value)


def solution(mesh):
    return jax.shard_map(
        functools.partial(local, mesh.shape["vel"]),
        mesh=mesh,
        in_specs=(P("vel", "groups", None), P("vel", None), P(), P()),
        out_specs=(P("vel", "groups", None), P("groups", None)),
        check_vma=False,
    )
```

time: 285 us -> 192 us (0.67)
  waiting for transfers between devices: 195 us -> 90.9 us
  blocking collectives: 0 us -> 63.2 us
  matrix products: 48.5 us -> 0 us
  Pallas kernels: 0 us -> 18.3 us
  other arithmetic: 13.9 us -> 2.41 us
  local copies, waits for them, and re-layouts: 12.3 us -> 2.78 us
    all_gather x1 -> x0, waiting for transfers between devices: 105 us -> none  [local(): gathered = lax.all_gather(epoch_maps, 'vel', axis=0, tiled=True)]
    dot_general x8 -> x0, matrix products: 48.5 us -> none  [one_block(): jnp.einsum('pvmoj,pvcj->vmoc', rows_done, column_band, preferred_element_...]
    all_to_all x0 -> x1, blocking collectives: none -> 39.6 us  [local(): received = lax.all_to_all(partial, 'vel', 0, 0, tiled=True)]
    all_gather x0 -> x1, blocking collectives: none -> 23.6 us  [local(): vels = lax.all_gather(velocity, 'vel', axis=0, tiled=True)]
    pallas_call x0 -> x1, Pallas kernels: none -> 18.3 us  [local(): pl.pallas_call(functools.partial(stack_kernel, count, rows, cols), out_sh...]
    slice x8 -> x0, local copies, waits for them, and re-layouts: 10.7 us -> none  [shift_bands(): rate_rows[None, :, 0]]
    select_n x8 -> x1, other arithmetic: 10.9 us -> 0.73 us  [local(): times = epoch_time[slots]]
  transfers between devices with their start and end apart: 2 -> 1, of which waited for: 2 -> 1; matrix products, arithmetic and copies ran while one was open for 0% -> 0% of each run, Pallas kernels for 0% -> 0%
where the time goes in v1:
time: 192 us
  waiting for transfers between devices  90.9 us (47%)
  blocking collectives  63.2 us (33%)
  Pallas kernels  18.3 us (10%)
  between operations  14.1 us (7%)
  local copies, waits for them, and re-layouts  2.78 us (1%)
  other arithmetic  2.41 us (1%)
    pmax x1, waiting for transfers between devices, local(): best_value = lax.pmax(jnp.max(likelihood, axis=0), 'vel')  90.9 us
    all_to_all x1, blocking collectives, local(): received = lax.all_to_all(partial, 'vel', 0, 0, tiled=True)  39.6 us
    all_gather x1, blocking collectives, local(): vels = lax.all_gather(velocity, 'vel', axis=0, tiled=True)  23.6 us
    pallas_call x1, Pallas kernels, local(): pl.pallas_call(functools.partial(stack_kernel, count, rows, cols), out_sh...  18.3 us
  transfers between devices with their start and end apart: 1, of which 1 were waited for; matrix products, arithmetic and copies ran while one was open for 0% of the time, Pallas kernels for 0%

profile of v1, /device:TPU:0, one launch (start us, length us, event | category | flops | bytes accessed | tf_op | source)
XLA Modules:
  0.0 191.6 jit_solution(3862846378550666099)
XLA Ops:
  7.2 0.0 copy-start
  7.2 0.0 all-reduce.2.cloned.1.call-start
  7.2 0.7 compare_select_fusion
  8.0 23.6 %all-gather = s32[16,1,2]{2,1,0:T(1,128)} all-gather(s32[1,1,2]{2,1,0:T(1,128)} %bitcast.8), channel_id=1, replica_groups=mesh['groups'=2,'vel'=16] {'vel'}, dimensions={0}, use_global_device_ids=true | all-gather | bytes 136 | tf_op jit(solution)/shard_map/all_gather | solution.py:109
  31.6 0.0 copy-done
  31.6 1.2 gather_fusion
  32.8 18.3 %shard_map.59 = bf16[16,96,512]{2,1,0:T(8,128)(2,1)} custom-call(s32[16,2]{1,0:T(8,128)} %bitcast.7, s32[8]{0:T(128)} %gather_fusion, bf16[8,96,512]{2,1,0:T(8,128)(2,1)} %images.1), custom_call_target="tpu_custom_call" | custom-call | tf_op jit(solution)/shard_map/pallas_call | solution.py:113
  51.0 39.6 %all_to_all.5 = bf16[16,96,512]{2,1,0:T(8,128)(2,1)S(1)} all-to-all(bf16[16,96,512]{2,1,0:T(8,128)(2,1)} %shard_map.59), channel_id=1, replica_groups=mesh['groups'=2,'vel'=16] {'vel'}, dimensions={0} | all-to-all | bytes 3145728 | tf_op jit(solution)/shard_map/all_to_all | solution.py:129
  90.6 0.2 convert_reduce_fusion
  90.9 0.7 fusion.2
  91.6 0.0 all-reduce.2.cloned.1.call-update
  91.6 0.7 fusion.1
  92.3 90.9 %all-reduce.2.cloned.1.call-done = f32[96,512]{1,0:T(8,128)} async-done(((f32[96,512]{1,0:T(8,128)}), f32[96,512]{1,0:T(8,128)}) %all-reduce.2.cloned.1.call-update) | async-done | bytes 196624 | tf_op jit(solution)/shard_map/pmax | solution.py:133
  183.2 1.6 copy.14
  (2 shorter events, 0.0 us)
Async XLA Ops:
  7.2 24.4 %copy-start = (s32[64]{0:T(128)S(1)}, s32[64]{0:T(128)}, u32[]{:S(2)}) copy-start(s32[64]{0:T(128)} %param.7) | copy-start | bytes 772
  7.2 176.0 %all-reduce.2.cloned.1.call-start = ((), (), s32[]{:S(2)}) async-start(), calls=%async_computation.1 | async-start | bytes 393216 | tf_op jit(solution)/shard_map/pmax | solution.py:133
Sparse Core Ops, SparseCore 0:
  91.7 91.4 all-reduce.1

commit v2 on v1

--- a/solution.py
+++ b/solution.py
@@ -102,9 +102,275 @@
             )
 
 
+def fused_kernel(
+    chips,
+    epochs,
+    count,
+    rows,
+    cols,
+    se_ref,
+    et_ref,
+    vel_ref,
+    images,
+    like_out,
+    best_out,
+    peer_images,
+    padded,
+    bands,
+    rows_done,
+    vel_all,
+    vel_smem,
+    part_send,
+    part_recv,
+    like_send,
+    max_send,
+    max_recv,
+    best_send,
+    local_sem,
+    image_sems,
+    vel_send,
+    vel_recv,
+    part_ssem,
+    part_rsem,
+    max_sems,
+    like_ssem,
+    like_rsem,
+    best_ssem,
+    best_rsem,
+):
+    me = lax.axis_index("vel")
+    chip, core = me // 2, me % 2
+    sibling = chip * 2 + 1 - core
+    blocks = cols // LANES
+    slice_rows = rows * blocks // chips
+    row0 = pl.multiple_of(chip // blocks * slice_rows, slice_rows)
+    col0 = pl.multiple_of(chip % blocks * LANES, LANES)
+
+    def remote(source, target, send, receive, device):
+        return pltpu.make_async_remote_copy(
+            src_ref=source,
+            dst_ref=target,
+            send_sem=send,
+            recv_sem=receive,
+            device_id={"vel": device},
+            device_id_type=pl.DeviceIdType.MESH,
+        )
+
+    def rail(step):
+        other = lax.rem(chip + step, chips)
+        return other, other * 2 + core
+
+    def each_rail(body):
+        @pl.loop(1, chips)
+        def _(step):
+            body(*rail(step))
+
+    barrier = pltpu.get_barrier_semaphore()
+    pl.semaphore_signal(
+        barrier, inc=1, device_id={"vel": sibling}, device_id_type=pl.DeviceIdType.MESH
+    )
+    each_rail(
+        lambda other, device: pl.semaphore_signal(
+            barrier, inc=1, device_id={"vel": device}, device_id_type=pl.DeviceIdType.MESH
+        )
+    )
+    pl.semaphore_wait(barrier, chips)
+
+    swap = remote(images, peer_images, image_sems.at[0], image_sems.at[1], sibling)
+    swap.start()
+
+    def vel_copy(other, device):
+        return remote(vel_ref, vel_all.at[chip], vel_send.at[other], vel_recv.at[chip], device)
+
+    each_rail(lambda other, device: vel_copy(other, device).start())
+    own = pltpu.make_async_copy(vel_ref, vel_all.at[chip], local_sem)
+    own.start()
+    pad_images(images, padded, count, rows, cols)
+    swap.wait_recv()
+    zeros = jnp.zeros((rows, HALO), jnp.bfloat16)
+    for s in range(count):
+        padded[count + s] = jnp.concatenate([zeros, peer_images[s], zeros], axis=1)
+    own.wait()
+
+    def vel_arrive(other, device):
+        remote(vel_ref, vel_all.at[other], vel_send.at[other], vel_recv.at[other], device).wait()
+
+    each_rail(vel_arrive)
+    to_smem = pltpu.make_async_copy(vel_all, vel_smem, local_sem)
+    to_smem.start()
+    to_smem.wait()
+
+    first = lax.rem(me * count, epochs)
+    peer_first = lax.rem(sibling * count, epochs)
+
+    def time(s):
+        slot = first + s if s < count else peer_first + (s - count)
+        return et_ref[se_ref[slot]]
+
+    @pl.loop(0, chips)
+    def _(v):
+        total = stack_one(
+            vel_smem[v, 0, 0],
+            vel_smem[v, 0, 1],
+            time,
+            padded,
+            bands,
+            rows_done,
+            2 * count,
+            rows,
+            cols,
+        ).astype(jnp.bfloat16)
+        for t in range(chips):
+            start = t % blocks * rows + t // blocks * slice_rows
+            part_send[t, v] = total[start : start + slice_rows]
+        part_recv[chip, v] = part_send[chip, v]
+        each_rail(
+            lambda other, device: remote(
+                part_send.at[other, v],
+                part_recv.at[chip, v],
+                part_ssem.at[other],
+                part_rsem.at[chip],
+                device,
+            ).start()
+        )
+
+    def part_arrive(other, device):
+        remote(
+            part_send.at[other], part_recv.at[other], part_ssem.at[other], part_rsem.at[other], device
+        ).wait()
+
+    each_rail(part_arrive)
+    best = None
+    for v in range(chips):
+        sums = []
+        for kind in range(2):
+            base = kind * (chips // 2)
+            acc = part_recv[base, v].astype(jnp.float32)
+            for source in range(1, chips // 2):
+                acc = acc + part_recv[base + source, v].astype(jnp.float32)
+            sums.append(acc / spline_norm)
+        value = sums[0] / jnp.sqrt(sums[1] + 1.0)
+        like_send[v] = value
+        best = value if best is None else jnp.maximum(best, value)
+    max_send[...] = best
+
+    meet = remote(max_send, max_recv, max_sems.at[0], max_sems.at[1], sibling)
+    meet.start()
+
+    window = (pl.ds(row0, slice_rows), pl.ds(col0, LANES))
+    each_rail(
+        lambda other, device: remote(
+            like_send.at[other],
+            like_out.at[0, window[0], window[1]],
+            like_ssem.at[other],
+            like_rsem.at[chip],
+            device,
+        ).start()
+    )
+    like_out[0, window[0], window[1]] = like_send[chip]
+    meet.wait()
+    best_send[...] = jnp.maximum(max_send[...], max_recv[...])
+    each_rail(
+        lambda other, device: remote(
+            best_send,
+            best_out.at[window[0], window[1]],
+            best_ssem.at[other],
+            best_rsem.at[chip],
+            device,
+        ).start()
+    )
+    best_out[window[0], window[1]] = best_send[...]
+
+    def finish(other, device):
+        theirs = (
+            pl.ds(pl.multiple_of(other // blocks * slice_rows, slice_rows), slice_rows),
+            pl.ds(pl.multiple_of(other % blocks * LANES, LANES), LANES),
+        )
+        remote(
+            like_send.at[other],
+            like_out.at[0, theirs[0], theirs[1]],
+            like_ssem.at[other],
+            like_rsem.at[other],
+            device,
+        ).wait()
+        remote(
+            best_send,
+            best_out.at[theirs[0], theirs[1]],
+            best_ssem.at[other],
+            best_rsem.at[other],
+            device,
+        ).wait()
+
+    each_rail(finish)
+    swap.wait_send()
+
+
+def fused(n, epoch_maps, velocity, slot_epoch, epoch_time):
+    count, rows, cols = epoch_maps.shape
+    epochs = slot_epoch.shape[0]
+    chips = n // 2
+    slice_rows = rows * (cols // LANES) // chips
+    vel_tile = jnp.broadcast_to(jnp.pad(velocity, ((0, 0), (0, LANES - 2))), (8, LANES))
+    smem = pl.BlockSpec(memory_space=pltpu.SMEM)
+    vmem = pl.BlockSpec(memory_space=pltpu.VMEM)
+    f32, bf16 = jnp.float32, jnp.bfloat16
+    dma = pltpu.SemaphoreType.DMA
+    return pl.pallas_call(
+        functools.partial(fused_kernel, chips, epochs, count, rows, cols),
+        out_shape=(
+            jax.ShapeDtypeStruct((1, rows, cols), f32),
+            jax.ShapeDtypeStruct((rows, cols), f32),
+        ),
+        in_specs=[smem, smem, vmem, vmem],
+        out_specs=(vmem, vmem),
+        scratch_shapes=[
+            pltpu.VMEM((count, rows, cols), bf16),
+            pltpu.VMEM((2 * count, rows, cols + 2 * HALO), bf16),
+            pltpu.VMEM((2 * count * 2 * LANES, LANES), bf16),
+            pltpu.VMEM((2 * count, rows, cols + 2 * HALO), bf16),
+            pltpu.VMEM((chips, 8, LANES), jnp.int32),
+            pltpu.SMEM((chips, 8, LANES), jnp.int32),
+            pltpu.VMEM((chips, chips, slice_rows, LANES), bf16),
+            pltpu.VMEM((chips, chips, slice_rows, LANES), bf16),
+            pltpu.VMEM((chips, slice_rows, LANES), f32),
+            pltpu.VMEM((slice_rows, LANES), f32),
+            pltpu.VMEM((slice_rows, LANES), f32),
+            pltpu.VMEM((slice_rows, LANES), f32),
+            dma,
+            dma((2,)),
+            dma((chips,)),
+            dma((chips,)),
+            dma((chips,)),
+            dma((chips,)),
+            dma((2,)),
+            dma((chips,)),
+            dma((chips,)),
+            dma((chips,)),
+            dma((chips,)),
+        ],
+        compiler_params=pltpu.CompilerParams(collective_id=0, has_side_effects=True),
+    )(slot_epoch, epoch_time, vel_tile, epoch_maps)
+
+
+def fits(n, epoch_maps, velocity, epochs):
+    count, rows, cols = epoch_maps.shape
+    chips = n // 2
+    blocks = cols // LANES
+    return (
+        n % 4 == 0
+        and velocity.shape[0] == 1
+        and n * count == 2 * epochs
+        and cols % LANES == 0
+        and chips % blocks == 0
+        and rows % (chips // blocks * 16) == 0
+    )
+
+
 def local(n, epoch_maps, velocity, slot_epoch, epoch_time):
     count, rows, cols = epoch_maps.shape
     epochs = slot_epoch.shape[0]
+    if fits(n, epoch_maps, velocity, epochs):
+        return fused(n, epoch_maps, velocity, slot_epoch, epoch_time)
     me = lax.axis_index("vel")
     vels = lax.all_gather(velocity, "vel", axis=0, tiled=True)
     first = lax.rem(me * count, epochs)

time: 192 us -> 47.7 us (0.25)
  waiting for transfers between devices: 90.9 us -> 0 us
  blocking collectives: 63.2 us -> 0 us
  Pallas kernels: 18.3 us -> 43.3 us
  between operations: 14.1 us -> 0.65 us
  other arithmetic: 2.41 us -> 0 us
    pmax x1 -> x0, waiting for transfers between devices: 90.9 us -> none  [local(): best_value = lax.pmax(jnp.max(likelihood, axis=0), 'vel')]
    all_to_all x1 -> x0, blocking collectives: 39.6 us -> none  [local(): received = lax.all_to_all(partial, 'vel', 0, 0, tiled=True)]
    pallas_call x1, Pallas kernels: 18.3 us -> 43.3 us  [fused(): pl.pallas_call(functools.partial(fused_kernel, chips, epochs, count, rows...]
    all_gather x1 -> x0, blocking collectives: 23.6 us -> none  [local(): vels = lax.all_gather(velocity, 'vel', axis=0, tiled=True)]
  transfers between devices with their start and end apart: 1 -> 0, of which waited for: 1 -> 0; matrix products, arithmetic and copies ran while one was open for 0% -> 0% of each run, Pallas kernels for 0% -> 0%
where the time goes in v2:
time: 47.7 us; the launch traced here: 47.5 us
  Pallas kernels  43.3 us (91%)
  local copies, waits for them, and re-layouts  3.59 us (8%)
  between operations  0.65 us (1%)
    pallas_call x1, Pallas kernels, fused(): pl.pallas_call(functools.partial(fused_kernel, chips, epochs, count, rows...  43.3 us
    unnamed x4, local copies, waits for them, and re-layouts  2.34 us
    broadcast_in_dim x2, local copies, waits for them, and re-layouts, fused(): jnp.broadcast_to(jnp.pad(velocity, ((0, 0), (0, LANES - 2))), (8, LANES))  1.26 us

profile of v2, /device:TPU:0, one launch (start us, length us, event | category | flops | bytes accessed | tf_op | source)
XLA Modules:
  0.0 47.5 jit_solution(4718549815619728669)
XLA Ops:
  0.6 0.7 %pad_bitcast_fusion = s32[128]{0:T(128)S(1)} fusion(s32[1,2]{1,0:T(1,128)} %param.5), kind=kLoop, calls=%fused_computation | loop fusion | bytes 520 | tf_op jit(solution)/shard_map/broadcast_in_dim | solution.py:313
  1.3 0.6 %broadcast_in_dim.8.vel_ref = s32[8,128]{1,0:T(8,128)} broadcast(s32[128]{0:T(128)S(1)} %pad_bitcast_fusion), dimensions={1} | broadcast | bytes 4608 | tf_op jit(solution)/shard_map/broadcast_in_dim | solution.py:313
  1.9 43.3 %shard_map.59 = (f32[1,96,512]{2,1,0:T(8,128)}, f32[96,512]{1,0:T(8,128)}) custom-call(s32[64]{0:T(128)} %se_ref.1, s32[64]{0:T(128)} %et_ref.1, s32[8,128]{1,0:T(8,128)} %broadcast_in_dim.8.vel_ref, bf16[8,96,512]{2,1,0:T(8,128)(2,1)} %images.1), custom_call_target="tpu_custom_call" | custom-call | tf_op jit(solution)/shard_map/pallas_call | solution.py:318
  45.2 0.0 copy-start
  45.2 1.7 %copy.8 = f32[1,96,512]{2,1,0:T(8,128)} copy(f32[1,96,512]{2,1,0:T(8,128)} %get-tuple-element.4) | data formatting | bytes 393216
  46.8 0.0 copy-done
  46.8 0.7 %copy.9 = f32[96,512]{1,0:T(8,128)} copy(f32[96,512]{1,0:T(8,128)S(1)} %copy-done) | data formatting | bytes 393216
Async XLA Ops:
  45.2 1.7 %copy-start = (f32[96,512]{1,0:T(8,128)S(1)}, f32[96,512]{1,0:T(8,128)}, u32[]{:S(2)}) copy-start(f32[96,512]{1,0:T(8,128)} %get-tuple-element.5) | copy-start | bytes 589828

commit v3 on v2

--- a/solution.py
+++ b/solution.py
@@ -73,14 +73,14 @@
     return jnp.dot(lhs, bands[...], preferred_element_type=jnp.float32)
 
 
-def pad_images(images, padded, count, rows, cols):
-    zeros = jnp.zeros((rows, HALO), jnp.bfloat16)
+def pad_images(images, padded, start, count):
+    zeros = jnp.zeros((images.shape[1], HALO), jnp.bfloat16)
     for s in range(count):
-        padded[s] = jnp.concatenate([zeros, images[s], zeros], axis=1)
+        padded[start + s] = jnp.concatenate([zeros, images[s], zeros], axis=1)
 
 
 def stack_kernel(count, rows, cols, vel_ref, time_ref, images, out, padded, bands, rows_done):
-    pad_images(images, padded, count, rows, cols)
+    pad_images(images, padded, 0, count)
     hypotheses = out.shape[0]
 
     @pl.loop(0, hypotheses)
@@ -119,19 +119,22 @@
     bands,
     rows_done,
     vel_all,
-    vel_smem,
     part_send,
     part_recv,
+    far_own,
+    hop_recv,
+    far_send,
     like_send,
     max_send,
     max_recv,
     best_send,
-    local_sem,
     image_sems,
     vel_send,
     vel_recv,
     part_ssem,
     part_rsem,
+    hop_ssem,
+    hop_rsem,
     max_sems,
     like_ssem,
     like_rsem,
@@ -142,9 +145,20 @@
     chip, core = me // 2, me % 2
     sibling = chip * 2 + 1 - core
     blocks = cols // LANES
+    half, quarter = chips // 2, chips // 4
     slice_rows = rows * blocks // chips
-    row0 = pl.multiple_of(chip // blocks * slice_rows, slice_rows)
-    col0 = pl.multiple_of(chip % blocks * LANES, LANES)
+    near0 = chip // half * half
+    far0 = half - near0
+    group = chip // quarter
+    inner = (group + 1) // 2 % 2
+    partner = chip + quarter * (1 - 2 * (group % 2))
+    far_inner = quarter * (2 - chip // half)
+
+    def window(owner):
+        return (
+            pl.ds(pl.multiple_of(owner // blocks * slice_rows, slice_rows), slice_rows),
+            pl.ds(pl.multiple_of(owner % blocks * LANES, LANES), LANES),
+        )
 
     def remote(source, target, send, receive, device):
         return pltpu.make_async_remote_copy(
@@ -156,49 +170,42 @@
             device_id_type=pl.DeviceIdType.MESH,
         )
 
-    def rail(step):
-        other = lax.rem(chip + step, chips)
-        return other, other * 2 + core
+    def rail(other):
+        return other * 2 + core
 
     def each_rail(body):
         @pl.loop(1, chips)
         def _(step):
-            body(*rail(step))
+            body(lax.rem(chip + step, chips))
+
+    def each_near(body):
+        @pl.loop(1, half)
+        def _(step):
+            body(near0 + lax.rem(chip - near0 + step, half))
+
+    def greet(device):
+        pl.semaphore_signal(
+            barrier, inc=1, device_id={"vel": device}, device_id_type=pl.DeviceIdType.MESH
+        )
 
     barrier = pltpu.get_barrier_semaphore()
-    pl.semaphore_signal(
-        barrier, inc=1, device_id={"vel": sibling}, device_id_type=pl.DeviceIdType.MESH
-    )
-    each_rail(
-        lambda other, device: pl.semaphore_signal(
-            barrier, inc=1, device_id={"vel": device}, device_id_type=pl.DeviceIdType.MESH
-        )
-    )
+    greet(sibling)
+    each_rail(lambda other: greet(rail(other)))
+    pad_images(images, padded, 0, count)
+    max_send[...] = jnp.full_like(max_send, -jnp.inf)
     pl.semaphore_wait(barrier, chips)
 
+    def vel_copy(source, target, other):
+        return remote(vel_ref, vel_all.at[target], vel_send.at[source], vel_recv.at[target], rail(other))
+
+    each_rail(lambda other: vel_copy(other, chip, other).start())
     swap = remote(images, peer_images, image_sems.at[0], image_sems.at[1], sibling)
     swap.start()
-
-    def vel_copy(other, device):
-        return remote(vel_ref, vel_all.at[chip], vel_send.at[other], vel_recv.at[chip], device)
-
-    each_rail(lambda other, device: vel_copy(other, device).start())
-    own = pltpu.make_async_copy(vel_ref, vel_all.at[chip], local_sem)
-    own.start()
-    pad_images(images, padded, count, rows, cols)
+    vel_all[chip, 0, 0] = vel_ref[0, 0]
+    vel_all[chip, 0, 1] = vel_ref[0, 1]
     swap.wait_recv()
-    zeros = jnp.zeros((rows, HALO), jnp.bfloat16)
-    for s in range(count):
-        padded[count + s] = jnp.concatenate([zeros, peer_images[s], zeros], axis=1)
-    own.wait()
-
-    def vel_arrive(other, device):
-        remote(vel_ref, vel_all.at[other], vel_send.at[other], vel_recv.at[other], device).wait()
-
-    each_rail(vel_arrive)
-    to_smem = pltpu.make_async_copy(vel_all, vel_smem, local_sem)
-    to_smem.start()
-    to_smem.wait()
+    pad_images(peer_images, padded, count, count)
+    each_rail(lambda other: vel_copy(other, other, other).wait())
 
     first = lax.rem(me * count, epochs)
     peer_first = lax.rem(sibling * count, epochs)
@@ -207,11 +214,85 @@
         slot = first + s if s < count else peer_first + (s - count)
         return et_ref[se_ref[slot]]
 
+    def part_copy(v, source, other):
+        return remote(
+            part_send.at[v, other],
+            part_recv.at[v, source],
+            part_ssem.at[v, other],
+            part_rsem.at[v, source],
+            rail(other),
+        )
+
+    def far_copy(v, step, source):
+        other = far0 + step
+        return remote(
+            far_send.at[v, step],
+            part_recv.at[v, source],
+            part_ssem.at[v, other],
+            part_rsem.at[v, source],
+            rail(other),
+        )
+
+    def hop_copy(v):
+        return remote(
+            part_send.at[v, pl.ds(far0, half)],
+            hop_recv.at[v],
+            hop_ssem.at[v],
+            hop_rsem.at[v],
+            rail(partner),
+        )
+
+    def like_copy(v, owner):
+        return remote(
+            like_send.at[v],
+            like_out.at[0, window(owner)[0], window(owner)[1]],
+            like_ssem.at[v],
+            like_rsem.at[owner],
+            rail(v),
+        )
+
+    def forward(v):
+        @pl.when(inner == 1)
+        def _():
+            hop_copy(v).wait_recv()
+
+            @pl.loop(0, half)
+            def _(step):
+                total = far_own[v % 2, far0 + step] + hop_recv[v, step].astype(jnp.float32)
+                far_send[v, step] = total.astype(jnp.bfloat16)
+                far_copy(v, step, chip).start()
+
+    def finish_like(v):
+        each_near(lambda other: part_copy(v, other, other).wait_recv())
+
+        @pl.loop(0, quarter)
+        def _(step):
+            far_copy(v, 0, far_inner + step).wait_recv()
+
+        near = part_recv[v, near0].astype(jnp.float32)
+        for step in range(1, half):
+            near = near + part_recv[v, near0 + step].astype(jnp.float32)
+        far = part_recv[v, far_inner].astype(jnp.float32)
+        for step in range(1, quarter):
+            far = far + part_recv[v, far_inner + step].astype(jnp.float32)
+        first_kind = near0 == 0
+        signal = jnp.where(first_kind, near, far) / spline_norm
+        weight = jnp.where(first_kind, far, near) / spline_norm
+        value = signal / jnp.sqrt(weight + 1.0)
+        max_send[...] = jnp.maximum(max_send[...], value)
+        like_send[v] = value
+
+        @pl.when(v != chip)
+        def _():
+            like_copy(v, chip).start()
+
+    late = 3
+
     @pl.loop(0, chips)
     def _(v):
         total = stack_one(
-            vel_smem[v, 0, 0],
-            vel_smem[v, 0, 1],
+            vel_all[v, 0, 0],
+            vel_all[v, 0, 1],
             time,
             padded,
             bands,
@@ -219,98 +300,81 @@
             2 * count,
             rows,
             cols,
-        ).astype(jnp.bfloat16)
+        )
         for t in range(chips):
             start = t % blocks * rows + t // blocks * slice_rows
-            part_send[t, v] = total[start : start + slice_rows]
-        part_recv[chip, v] = part_send[chip, v]
-        each_rail(
-            lambda other, device: remote(
-                part_send.at[other, v],
-                part_recv.at[chip, v],
-                part_ssem.at[other],
-                part_rsem.at[chip],
-                device,
-            ).start()
-        )
-
-    def part_arrive(other, device):
-        remote(
-            part_send.at[other], part_recv.at[other], part_ssem.at[other], part_rsem.at[other], device
-        ).wait()
-
-    each_rail(part_arrive)
-    best = None
-    for v in range(chips):
-        sums = []
-        for kind in range(2):
-            base = kind * (chips // 2)
-            acc = part_recv[base, v].astype(jnp.float32)
-            for source in range(1, chips // 2):
-                acc = acc + part_recv[base + source, v].astype(jnp.float32)
-            sums.append(acc / spline_norm)
-        value = sums[0] / jnp.sqrt(sums[1] + 1.0)
-        like_send[v] = value
-        best = value if best is None else jnp.maximum(best, value)
-    max_send[...] = best
+            piece = total[start : start + slice_rows]
+            far_own[v % 2, t] = piece
+            part_send[v, t] = piece.astype(jnp.bfloat16)
+        part_recv[v, chip] = part_send[v, chip]
+
+        @pl.when(inner == 0)
+        def _():
+            hop_copy(v).start()
+
+        each_near(lambda other: part_copy(v, chip, other).start())
+
+        @pl.when(v >= 1)
+        def _():
+            forward(v - 1)
+
+        @pl.when(v >= late)
+        def _():
+            finish_like(v - late)
+
+    forward(chips - 1)
+
+    @pl.loop(chips - late, chips)
+    def _(v):
+        finish_like(v)
 
     meet = remote(max_send, max_recv, max_sems.at[0], max_sems.at[1], sibling)
     meet.start()
-
-    window = (pl.ds(row0, slice_rows), pl.ds(col0, LANES))
-    each_rail(
-        lambda other, device: remote(
-            like_send.at[other],
-            like_out.at[0, window[0], window[1]],
-            like_ssem.at[other],
-            like_rsem.at[chip],
-            device,
-        ).start()
-    )
-    like_out[0, window[0], window[1]] = like_send[chip]
+    like_out[0, window(chip)[0], window(chip)[1]] = like_send[chip]
     meet.wait()
     best_send[...] = jnp.maximum(max_send[...], max_recv[...])
-    each_rail(
-        lambda other, device: remote(
+
+    def best_copy(owner, other):
+        return remote(
             best_send,
-            best_out.at[window[0], window[1]],
+            best_out.at[window(owner)[0], window(owner)[1]],
             best_ssem.at[other],
-            best_rsem.at[chip],
-            device,
-        ).start()
-    )
-    best_out[window[0], window[1]] = best_send[...]
-
-    def finish(other, device):
-        theirs = (
-            pl.ds(pl.multiple_of(other // blocks * slice_rows, slice_rows), slice_rows),
-            pl.ds(pl.multiple_of(other % blocks * LANES, LANES), LANES),
-        )
-        remote(
-            like_send.at[other],
-            like_out.at[0, theirs[0], theirs[1]],
-            like_ssem.at[other],
-            like_rsem.at[other],
-            device,
-        ).wait()
-        remote(
-            best_send,
-            best_out.at[theirs[0], theirs[1]],
-            best_ssem.at[other],
-            best_rsem.at[other],
-            device,
-        ).wait()
+            best_rsem.at[owner],
+            rail(other),
+        )
+
+    each_rail(lambda other: best_copy(chip, other).start())
+    best_out[window(chip)[0], window(chip)[1]] = best_send[...]
+
+    @pl.loop(0, chips)
+    def _(v):
+        each_near(lambda other: part_copy(v, chip, other).wait_send())
+
+        @pl.when(inner == 0)
+        def _():
+            hop_copy(v).wait_send()
+
+        @pl.when(inner == 1)
+        def _():
+            @pl.loop(0, half)
+            def _(step):
+                far_copy(v, step, chip).wait_send()
+
+    swap.wait_send()
+
+    def finish(other):
+        like_copy(other, other).wait()
+        best_copy(other, other).wait()
 
     each_rail(finish)
-    swap.wait_send()
 
 
 def fused(n, epoch_maps, velocity, slot_epoch, epoch_time):
     count, rows, cols = epoch_maps.shape
     epochs = slot_epoch.shape[0]
     chips = n // 2
+    half = chips // 2
     slice_rows = rows * (cols // LANES) // chips
-    vel_tile = jnp.broadcast_to(jnp.pad(velocity, ((0, 0), (0, LANES - 2))), (8, LANES))
     smem = pl.BlockSpec(memory_space=pltpu.SMEM)
     vmem = pl.BlockSpec(memory_space=pltpu.VMEM)
     f32, bf16 = jnp.float32, jnp.bfloat16
@@ -321,25 +385,28 @@
             jax.ShapeDtypeStruct((1, rows, cols), f32),
             jax.ShapeDtypeStruct((rows, cols), f32),
         ),
-        in_specs=[smem, smem, vmem, vmem],
+        in_specs=[smem, smem, smem, vmem],
         out_specs=(vmem, vmem),
         scratch_shapes=[
             pltpu.VMEM((count, rows, cols), bf16),
             pltpu.VMEM((2 * count, rows, cols + 2 * HALO), bf16),
             pltpu.VMEM((2 * count * 2 * LANES, LANES), bf16),
             pltpu.VMEM((2 * count, rows, cols + 2 * HALO), bf16),
-            pltpu.VMEM((chips, 8, LANES), jnp.int32),
-            pltpu.SMEM((chips, 8, LANES), jnp.int32),
+            pltpu.SMEM((chips, 1, 2), jnp.int32),
             pltpu.VMEM((chips, chips, slice_rows, LANES), bf16),
             pltpu.VMEM((chips, chips, slice_rows, LANES), bf16),
+            pltpu.VMEM((2, chips, slice_rows, LANES), f32),
+            pltpu.VMEM((chips, half, slice_rows, LANES), bf16),
+            pltpu.VMEM((chips, half, slice_rows, LANES), bf16),
             pltpu.VMEM((chips, slice_rows, LANES), f32),
             pltpu.VMEM((slice_rows, LANES), f32),
             pltpu.VMEM((slice_rows, LANES), f32),
             pltpu.VMEM((slice_rows, LANES), f32),
-            dma,
             dma((2,)),
             dma((chips,)),
             dma((chips,)),
+            dma((chips, chips)),
+            dma((chips, chips)),
             dma((chips,)),
             dma((chips,)),
             dma((2,)),
@@ -349,7 +416,7 @@
             dma((chips,)),
         ],
         compiler_params=pltpu.CompilerParams(collective_id=0, has_side_effects=True),
-    )(slot_epoch, epoch_time, vel_tile, epoch_maps)
+    )(slot_epoch, epoch_time, velocity, epoch_maps)
 
 
 def fits(n, epoch_maps, velocity, epochs):

time: 47.7 us -> 46.3 us (0.971)
  local copies, waits for them, and re-layouts: 3.59 us -> 2.34 us
    broadcast_in_dim x2 -> x0, local copies, waits for them, and re-layouts: 1.26 us -> none  [fused(): jnp.broadcast_to(jnp.pad(velocity, ((0, 0), (0, LANES - 2))), (8, LANES))]
where the time goes in v3:
time: 46.3 us; the launch traced here: 46.1 us
  Pallas kernels  43.2 us (93%)
  local copies, waits for them, and re-layouts  2.34 us (5%)
  between operations  0.65 us (1%)
    pallas_call x1, Pallas kernels, fused(): pl.pallas_call(functools.partial(fused_kernel, chips, epochs, count, rows...  43.2 us
    unnamed x4, local copies, waits for them, and re-layouts  2.34 us

profile of v3, /device:TPU:0, one launch (start us, length us, event | category | flops | bytes accessed | tf_op | source)
XLA Modules:
  0.0 46.1 jit_solution(13334042201149502794)
XLA Ops:
  0.6 43.2 %shard_map.59 = (f32[1,96,512]{2,1,0:T(8,128)}, f32[96,512]{1,0:T(8,128)}) custom-call(s32[64]{0:T(128)} %se_ref.1, s32[64]{0:T(128)} %et_ref.1, s32[1,2]{1,0:T(1,128)} %vel_ref.1, bf16[8,96,512]{2,1,0:T(8,128)(2,1)} %images.1), custom_call_target="tpu_custom_call" | custom-call | tf_op jit(solution)/shard_map/pallas_call | solution.py:382
  43.8 0.0 copy-start
  43.8 1.7 %copy.8 = f32[1,96,512]{2,1,0:T(8,128)} copy(f32[1,96,512]{2,1,0:T(8,128)} %get-tuple-element.4) | data formatting | bytes 393216
  45.5 0.0 copy-done
  45.5 0.7 %copy.9 = f32[96,512]{1,0:T(8,128)} copy(f32[96,512]{1,0:T(8,128)S(1)} %copy-done) | data formatting | bytes 393216
Async XLA Ops:
  43.8 1.7 %copy-start = (f32[96,512]{1,0:T(8,128)S(1)}, f32[96,512]{1,0:T(8,128)}, u32[]{:S(2)}) copy-start(f32[96,512]{1,0:T(8,128)} %get-tuple-element.5) | copy-start | bytes 589828

commit v4 on v3

--- a/solution.py
+++ b/solution.py
@@ -112,8 +112,7 @@
     et_ref,
     vel_ref,
     images,
-    like_out,
-    best_out,
+    out_ref,
     peer_images,
     padded,
     bands,
@@ -141,6 +140,7 @@
     best_ssem,
     best_rsem,
 ):
+    like_out, best_out = out_ref.at[pl.ds(0, 1)], out_ref.at[1]
     me = lax.axis_index("vel")
     chip, core = me // 2, me % 2
     sibling = chip * 2 + 1 - core
@@ -379,14 +379,11 @@
     vmem = pl.BlockSpec(memory_space=pltpu.VMEM)
     f32, bf16 = jnp.float32, jnp.bfloat16
     dma = pltpu.SemaphoreType.DMA
-    return pl.pallas_call(
+    both = pl.pallas_call(
         functools.partial(fused_kernel, chips, epochs, count, rows, cols),
-        out_shape=(
-            jax.ShapeDtypeStruct((1, rows, cols), f32),
-            jax.ShapeDtypeStruct((rows, cols), f32),
-        ),
+        out_shape=jax.ShapeDtypeStruct((2, rows, cols), f32),
         in_specs=[smem, smem, smem, vmem],
-        out_specs=(vmem, vmem),
+        out_specs=vmem,
         scratch_shapes=[
             pltpu.VMEM((count, rows, cols), bf16),
             pltpu.VMEM((2 * count, rows, cols + 2 * HALO), bf16),
@@ -417,6 +414,7 @@
         ],
         compiler_params=pltpu.CompilerParams(collective_id=0, has_side_effects=True),
     )(slot_epoch, epoch_time, velocity, epoch_maps)
+    return (both[:1], both[1])
 
 
 def fits(n, epoch_maps, velocity, epochs):

time: 46.3 us -> 45.7 us (0.987)
  local copies, waits for them, and re-layouts: 2.34 us -> 1.79 us
    unnamed x4 -> x0, local copies, waits for them, and re-layouts: 2.34 us -> none
    squeeze x0 -> x1, local copies, waits for them, and re-layouts: none -> 1.79 us  [fused(): return (both[:1], both[1])]
where the time goes in v4:
time: 45.7 us; the launch traced here: 45.6 us
  Pallas kernels  43.2 us (95%)
  local copies, waits for them, and re-layouts  1.79 us (4%)
  between operations  0.64 us (1%)
    pallas_call x1, Pallas kernels, fused(): pl.pallas_call(functools.partial(fused_kernel, chips, epochs, count, rows...  43.2 us
    squeeze x1, local copies, waits for them, and re-layouts, fused(): return (both[:1], both[1])  1.79 us

profile of v4, /device:TPU:0, one launch (start us, length us, event | category | flops | bytes accessed | tf_op | source)
XLA Modules:
  0.0 45.6 jit_solution(9606200665834610048)
XLA Ops:
  0.6 43.2 %shard_map.59 = f32[2,96,512]{2,1,0:T(8,128)} custom-call(s32[64]{0:T(128)} %se_ref.1, s32[64]{0:T(128)} %et_ref.1, s32[1,2]{1,0:T(1,128)} %vel_ref.1, bf16[8,96,512]{2,1,0:T(8,128)(2,1)} %images.1), custom_call_target="tpu_custom_call" | custom-call | tf_op jit(solution)/shard_map/pallas_call | solution.py:382
  43.8 1.8 %slice_bitcast_fusion = (f32[96,512]{1,0:T(8,128)}, f32[1,96,512]{2,1,0:T(8,128)}) fusion(f32[2,96,512]{2,1,0:T(8,128)} %shard_map.59), kind=kLoop, calls=%fused_computation | loop fusion | bytes 786432 | tf_op jit(solution)/shard_map/squeeze | solution.py:417
